TPU v7x, 512 devices: a whole 4x4x16 slice. The times are simulated.
512 devices in a mesh: obs: 8 (over x, core), dt: 64 (over y, z).
Axes of the slice: x: 4, y: 4, z: 16, core: 2. Of those that a mesh axis runs over, the one named last changes fastest.
Arguments:
- sky_map: float32 [512, 3, 512], P(('obs', 'dt')), may hold values from -6 to 6
- submap_of: int32 [8, 128, 16384], P('obs', None, 'dt'), may hold values from 0 to 511, as said below
- pixel_cell: int32 [8, 128, 16384], P('obs', None, 'dt'), may hold values from 0 to 511
- angles: float32 [8, 128, 16384], P('obs', None, 'dt'), may hold values from -3.140625 to 3.140625
- intervals: int32 [8, 16384], P('obs', 'dt'), may hold values from 0 to 31, never falling along the last dimension, each value on 1 to 1024 neighbouring positions
- wafer_of: int32 [8, 128], P('obs'), may hold values from 0 to 3
- mixing: bfloat16 [8, 128, 128], P('obs'), may hold values from -1 to 1
- knee: float32 [8, 128], P('obs'), may hold values from 2 to 200
Outputs:
- sky_out: float32 [512, 3, 512], P(('obs', 'dt'))
Inputs may be any that keep to these rules, and one draw needn't show every extreme that they name: `submap_of`: the submaps of observation o lie in o * 64 to (o + 2) * 64 - 1, counted modulo 512.
All inputs are finite; a program needn't handle non-finite values.
Results may differ from a plain program's by a relative error of at most 0.00097.
Values sent between devices are 32-bit elements; how exact they have to be, the bound alone decides.
A program may use at most 128 MiB of HBM per device.

v0:
```python
import math

import jax
import jax.numpy as jnp
from jax import lax
from jax.sharding import PartitionSpec as P


def passed_along(value, axis, steps):
    count = lax.axis_size(axis)
    pairs = [(source, (source + steps) % count) for source in range(count)]
    return lax.ppermute(value, axis, pairs)


def phase_table(first, second, modulus):
    product = first[:, None] * second[None, :] % modulus
    angle = 2.0 * math.pi / modulus * product.astype(jnp.float32)
    return (jnp.cos(angle), jnp.sin(angle))


def mult(form, left, right):
    return jnp.einsum(form, left, right, precision=lax.Precision.HIGHEST)


def noise_filter(series, knee_local):
    batch = series.shape[0]
    length = series.shape[1]
    n_one = 128
    n_two = length // n_one
    grid = series.reshape(batch, n_one, n_two)
    index_one = jnp.arange(n_one, dtype=jnp.int32)
    index_two = jnp.arange(n_two, dtype=jnp.int32)
    cos_one, sin_one = phase_table(index_one, index_one, n_one)
    cos_twid, sin_twid = phase_table(index_one, index_two, length)
    cos_two, sin_two = phase_table(index_two, index_two, n_two)
    first_re = mult("kn,bnm->bkm", cos_one, grid)
    first_im = -mult("kn,bnm->bkm", sin_one, grid)
    twid_re = first_re * cos_twid + first_im * sin_twid
    twid_im = first_im * cos_twid - first_re * sin_twid
    spec_re = mult("bkm,mj->bkj", twid_re, cos_two) + mult("bkm,mj->bkj", twid_im, sin_two)
    spec_im = mult("bkm,mj->bkj", twid_im, cos_two) - mult("bkm,mj->bkj", twid_re, sin_two)
    freq_index = index_one[:, None] + n_one * index_two[None, :]
    folded = jnp.minimum(freq_index, length - freq_index).astype(jnp.float32)
    weight = folded[None] ** 2 / (folded[None] ** 2 + knee_local[:, None, None] ** 2)
    spec_re = weight * spec_re
    spec_im = weight * spec_im
    back_re = mult("bkj,jm->bkm", spec_re, cos_two) - mult("bkj,jm->bkm", spec_im, sin_two)
    back_im = mult("bkj,jm->bkm", spec_re, sin_two) + mult("bkj,jm->bkm", spec_im, cos_two)
    turn_re = back_re * cos_twid - back_im * sin_twid
    turn_im = back_re * sin_twid + back_im * cos_twid
    result = mult("kn,bkm->bnm", cos_one, turn_re) - mult("kn,bkm->bnm", sin_one, turn_im)
    return (result / length).reshape(batch, length)


def body(sky_map, submap_of, pixel_cell, angles, intervals, wafer_of, mixing, knee):
    n_dt = lax.axis_size("dt")
    obs_index = lax.axis_index("obs")
    dt_index = lax.axis_index("dt")
    pix_sub = sky_map.shape[2]
    own_patch = lax.all_gather(sky_map, "dt", axis=0, tiled=True)
    next_patch = passed_along(own_patch, "obs", -1)
    patch = jnp.concatenate([own_patch, next_patch], axis=0)
    patch_pixels = 2 * n_dt * pix_sub
    table = jnp.transpose(patch, (1, 0, 2)).reshape(3, patch_pixels)
    all_submaps = lax.axis_size("obs") * n_dt
    local_submap = (submap_of[0] - obs_index * n_dt) % all_submaps
    local_index = local_submap * pix_sub + pixel_cell[0]
    sampled = table[:, local_index]
    cos_weight = jnp.cos(2.0 * angles[0])
    sin_weight = jnp.sin(2.0 * angles[0])
    keep_mask = (intervals[0] % 2 == 0).astype(jnp.float32)
    tod = keep_mask[None, :] * (sampled[0] + cos_weight * sampled[1] + sin_weight * sampled[2])
    wafers = wafer_of[0]
    same = wafers[:, None] == wafers[None, :]
    masked = jnp.where(same, mixing[0], jnp.zeros_like(mixing[0]))
    corr = tod + jnp.dot(masked, tod.astype(jnp.bfloat16), preferred_element_type=jnp.float32)
    det_major = lax.all_to_all(corr[None], "dt", split_axis=1, concat_axis=2, tiled=True)
    det_local = det_major.shape[1]
    knee_local = lax.dynamic_slice_in_dim(knee[0], dt_index * det_local, det_local, 0)
    filtered = noise_filter(det_major[0], knee_local)
    returned = lax.all_to_all(filtered[None], "dt", split_axis=2, concat_axis=1, tiled=True)[0]
    weighted = keep_mask[None, :] * returned
    contrib = jnp.stack([weighted, weighted * cos_weight, weighted * sin_weight]).reshape(3, -1)
    partial_value = (
        jnp.zeros((3, patch_pixels), jnp.float32).at[:, local_index.reshape(-1)].add(contrib)
    )
    partial_value = jnp.transpose(partial_value.reshape(3, 2, n_dt, pix_sub), (1, 2, 0, 3))
    own_part = partial_value[0]
    next_part = partial_value[1]
    arrived = passed_along(next_part, "obs", 1)
    sky_out = lax.psum_scatter(own_part + arrived, "dt", scatter_dimension=0, tiled=True)
    return sky_out


def solution(mesh):
    return jax.shard_map(
        body,
        mesh=mesh,
        in_specs=(
            P(("obs", "dt"), None, None),
            P("obs", None, "dt"),
            P("obs", None, "dt"),
            P("obs", None, "dt"),
            P("obs", "dt"),
            P("obs", None),
            P("obs", None, None),
            P("obs", None),
        ),
        out_specs=P(("obs", "dt"), None, None),
        check_vma=False,
    )
```

profile of v0, /device:TPU:6, one launch (start us, length us, event | category | flops | bytes accessed | tf_op | source)
XLA Modules:
  0.0 929.8 jit_solution(10198880908324625660)
XLA Ops:
  6.5 0.7 copy.44
  7.2 107.1 %all_gather.3 = f32[64,3,512]{2,1,0:T(4,128)S(1)} all-gather(f32[1,3,512]{2,1,0:T(4,128)S(1)} %copy.44), channel_id=1, replica_groups=mesh['obs'=8,'dt'=64] {'dt'}, dimensions={0}, use_global_device_ids=true | all-gather | bytes 399360 | tf_op jit(solution)/shard_map/all_gather | solution.py:60
  114.3 0.3 fusion.81
  114.6 1.0 fusion.12
  115.6 0.1 copy.83
  115.7 0.1 copy.50
  115.8 0.7 compare_convert_fusion
  116.5 0.9 subtract_bitcast_fusion
  117.5 3.6 collective-permute-done
  121.0 0.2 maximum_bitcast_fusion
  121.3 15.6 %copy.45 = f32[3,128,512]{0,2,1:T(8,128)} copy(f32[3,128,512]{2,0,1:T(4,128)S(1)} %maximum_bitcast_fusion) | data formatting | bytes 1572864 | tf_op jit(solution)/shard_map/transpose | solution.py:64
  136.9 118.8 %gather_fusion = f32[32768,3]{1,0:T(8,128)} fusion(f32[3,65536]{0,1:T(8,128)} %bitcast.110, s32[32768]{0:T(1024)S(1)} %broadcast_clamp_fusion), kind=kCustom, calls=%fused_computation | custom fusion | bytes 917504 | tf_op jit(solution)/shard_map/gather | solution.py:68
  255.7 10.0 %copy.77 = f32[128,256,3]{1,0,2:T(8,128)S(1)} copy(f32[128,256,3]{2,1,0:T(8,128)} %bitcast.113) | data formatting | bytes 786432 | tf_op jit(solution)/shard_map/gather | solution.py:68
  265.7 1.0 fusion.7
  266.7 0.8 copy.47
  267.5 9.9 %all-to-all-start = ((f32[1,128,256]{2,0,1:T(1,128)}), f32[1,128,256]{2,0,1:T(1,128)S(1)}, u32[]{:S(2)}, u32[]{:S(2)}) async-start(f32[1,128,256]{2,0,1:T(1,128)} %copy.47), calls=%async_computation | async-start | bytes 262144 | tf_op jit(solution)/shard_map/all_to_all | solution.py:77
  277.3 0.3 fusion.80
  277.6 0.1 copy.52
  277.7 0.1 copy.80
  277.8 0.1 copy.81
  278.0 0.1 multiply_bitcast_fusion.2
  278.1 15.5 %all-to-all-done = f32[1,128,256]{2,0,1:T(1,128)S(1)} async-done(((f32[1,128,256]{2,0,1:T(1,128)}), f32[1,128,256]{2,0,1:T(1,128)S(1)}, u32[]{:S(2)}, u32[]{:S(2)}) %all-to-all-start) | async-done | bytes 131104 | tf_op jit(solution)/shard_map/all_to_all | solution.py:77
  293.6 0.6 convolution_bitcast_fusion
  294.2 0.5 fusion.2
  294.7 0.6 fusion.43
  295.3 0.6 fusion.47
  295.9 0.6 fusion.3
  296.5 0.5 fusion.45
  297.0 0.6 fusion.35
  297.6 0.6 fusion.4
  298.2 0.6 convolution_subtract_fusion.1
  298.7 0.5 convolution_add_fusion
  299.3 0.5 fusion.21
  299.8 0.5 fusion.6
  300.3 7.5 copy.78
  307.8 0.5 broadcast.426
  308.3 74.5 %reduce = f32[16384,2]{1,0:T(8,128)} reduce(f32[16384,1,2]{2,1,0:T(1,128)} %bitcast.111, f32[]{:T(128)} %broadcast.426), dimensions={1}, to_apply=%bitcast.100.reduce_sub_computation | reduce | bytes 262148
  382.8 8.2 reshape.383
  391.0 6.4 all-to-all-start.1
  397.4 0.0 all-reduce.3.cloned.1.call-start
  397.4 0.5 compare_select_fusion
  398.0 0.1 copy.82
  398.1 15.5 %all-to-all-done.1 = f32[64,1,512]{2,1,0:T(1,128)S(1)} async-done(((f32[64,1,512]{2,1,0:T(1,128)}), f32[64,1,512]{2,1,0:T(1,128)S(1)}, u32[]{:S(2)}, u32[]{:S(2)}) %all-to-all-start.1) | async-done | bytes 131104 | tf_op jit(solution)/shard_map/all_to_all | solution.py:81
  413.6 1.0 reduce.1
  414.6 14.9 %reshape.384 = f32[16384,1,2]{2,1,0:T(1,128)} reshape(f32[64,512]{1,0:T(8,128)S(1)} %reduce.1) | data formatting | bytes 262144
  429.5 5.4 copy.63
  434.8 0.2 squeeze.27
  435.0 0.1 squeeze.28
  435.1 0.5 multiply_bitcast_fusion.1
  435.6 0.1 copy.84
  435.8 0.1 copy.85
  435.9 0.1 mul.376
  436.1 0.3 maximum_bitcast_fusion.1
  436.4 8.5 copy.64
  444.9 187.4 %scatter_custom_fusion = f32[3,65536]{0,1:T(8,128)} fusion(s32[32768]{0:T(1024)S(1)} %bitcast.128, f32[32768,3]{1,0:T(8,128)} %copy.64, f32[]{:T(128)} %constant.74.clone.1), kind=kCustom, calls=%fused_computation.2 | custom fusion | flops 98304 | bytes 786944 | tf_op jit(solution)/shard_map/scatter-add | solution.py:85
  632.3 17.5 %copy.65 = f32[3,2,64,512]{3,0,2,1:T(4,128)S(1)} copy(f32[3,2,64,512]{0,3,2,1:T(8,128)} %bitcast.109) | data formatting | bytes 1572864 | tf_op jit(solution)/shard_map/reshape | solution.py:87
  649.8 0.1 slice_bitcast_fusion
  649.9 0.0 collective-permute-start.1
  649.9 8.6 collective-permute-done.1
  658.5 0.9 fusion.8
  659.5 1.3 dynamic-slice.1
  660.7 260.3 %all-reduce.3.cloned.1.call-done = f32[64,3,512]{2,1,0:T(4,128)} async-done(((f32[64,3,512]{2,1,0:T(4,128)}), f32[64,3,512]{2,1,0:T(4,128)}) %all-reduce.3.cloned.1.call-update) | async-done | bytes 393232
  921.0 1.3 constant_dynamic-slice_fusion
  922.4 0.6 copy.66
  (18 shorter events, 0.1 us)
Async XLA Ops:
  114.3 6.7 collective-permute-start
  136.9 128.8 %copy-start.1 = (f32[1,128,256]{2,1,0:T(8,128)S(1)}, f32[1,128,256]{2,1,0:T(8,128)}, u32[]{:S(2)}) copy-start(f32[1,128,256]{2,1,0:T(8,128)} %param.11) | copy-start | bytes 393220
  136.9 128.8 %copy-start.2 = (bf16[1,128,128]{2,1,0:T(8,128)(2,1)S(1)}, bf16[1,128,128]{2,1,0:T(8,128)(2,1)}, u32[]{:S(2)}) copy-start(bf16[1,128,128]{2,1,0:T(8,128)(2,1)} %param.14) | copy-start | bytes 98308
  136.9 128.8 %copy-start.3 = (s32[1,128]{1,0:T(1,128)S(1)}, s32[1,128]{1,0:T(1,128)}, u32[]{:S(2)}) copy-start(s32[1,128]{1,0:T(1,128)} %param.13) | copy-start | bytes 1540
  136.9 141.0 %copy-start = (s32[1,128,256]{2,1,0:T(8,128)S(1)}, s32[1,128,256]{2,1,0:T(8,128)}, u32[]{:S(2)}) copy-start(s32[1,128,256]{2,1,0:T(8,128)} %param.10) | copy-start | bytes 393220
  136.9 141.1 %copy-start.4 = (f32[1,128]{1,0:T(1,128)S(1)}, f32[1,128]{1,0:T(1,128)}, u32[]{:S(2)}) copy-start(f32[1,128]{1,0:T(1,128)} %param.15) | copy-start | bytes 1540
  267.5 26.1 %all-to-all-start = ((f32[1,128,256]{2,0,1:T(1,128)}), f32[1,128,256]{2,0,1:T(1,128)S(1)}, u32[]{:S(2)}, u32[]{:S(2)}) async-start(f32[1,128,256]{2,0,1:T(1,128)} %copy.47), calls=%async_computation | async-start | bytes 262144 | tf_op jit(solution)/shard_map/all_to_all | solution.py:77
  391.0 22.6 %all-to-all-start.1 = ((f32[64,1,512]{2,1,0:T(1,128)}), f32[64,1,512]{2,1,0:T(1,128)S(1)}, u32[]{:S(2)}, u32[]{:S(2)}) async-start(f32[64,1,512]{2,1,0:T(1,128)} %reshape.383), calls=%async_computation.1 | async-start | bytes 262144 | tf_op jit(solution)/shard_map/all_to_all | solution.py:81
  397.4 523.7 %all-reduce.3.cloned.1.call-start = ((), (), s32[]{:S(2)}) async-start(), calls=%async_computation.2 | async-start | bytes 1048576
  649.9 8.6 collective-permute-start.1
Sparse Core Ops, SparseCore 0:
  659.6 261.4 all-reduce.2
where the time goes:
time: 931 us; the launch traced here: 930 us
  waiting for transfers between devices  303 us (33%)
  other arithmetic  269 us (29%)
  local copies, waits for them, and re-layouts  213 us (23%)
  blocking collectives  107 us (11%)
  starting transfers between devices  16.3 us (2%)
  between operations  13.8 us (1%)
    unnamed x2, waiting for transfers between devices  260 us
    scatter-add x1, other arithmetic, body(): jnp.zeros((3, patch_pixels), jnp.float32).at[:, local_index.reshape(-1)]  187 us
    gather x2, local copies, waits for them, and re-layouts, body(): sampled = table[:, local_index]  129 us
    all_gather x1, blocking collectives, body(): own_patch = lax.all_gather(sky_map, 'dt', axis=0, tiled=True)  107 us
    unnamed x4, other arithmetic  76.9 us
    unnamed x23, local copies, waits for them, and re-layouts  27.7 us
  transfers between devices with their start and end apart: 5, of which 5 were waited for; matrix products, arithmetic and copies ran while one was open for 1% of the time, Pallas kernels for 0%

commit v1 on v0

v1 whole, which is shorter than its diff:
```python
import math

import jax
import jax.numpy as jnp
import ml_dtypes
import numpy as np
from jax import lax
from jax.experimental import pallas as pl
from jax.experimental.pallas import tpu as pltpu
from jax.sharding import PartitionSpec as P

MESH = pl.DeviceIdType.MESH
f32, bf16, i32 = jnp.float32, jnp.bfloat16, jnp.int32

DET = 128
SPAN = 256
PIX = 512
GROUP = 64
NY, NZ = 4, 16
WINDOW = 2 * GROUP
NSAMP = GROUP * SPAN
TILE = 8


def split_np(x):
    high = x.astype(ml_dtypes.bfloat16)
    low = (x - high.astype(np.float64)).astype(ml_dtypes.bfloat16)
    return high, low


def dft_tables():
    n = 128
    row = np.arange(256)
    row_det, row_n1 = (row // 2) % 2, 2 * (row // 4) + row % 2
    col_det, col_k1 = row // n, row % n
    same = (row_det[:, None] == col_det[None, :]).astype(np.float64)
    turn = 2.0 * np.pi * ((row_n1[:, None] * col_k1[None, :]) % n) / n
    cos_part, sin_part = same * np.cos(turn), -same * np.sin(turn)
    last = np.concatenate([cos_part, sin_part], axis=1)
    first = np.ascontiguousarray(last.T)
    index = np.arange(n)
    angle = 2.0 * np.pi * ((index[:, None] * index[None, :]) % n) / n
    c, s = np.cos(angle), np.sin(angle)
    forward = np.block([[c, -s], [s, c]])
    backward = np.block([[c, s], [-s, c]]) / NSAMP
    twist = 2.0 * np.pi * (col_k1[:, None] * index[None, :]) / NSAMP
    tables = []
    for x in (first, forward, backward, last):
        tables.extend(split_np(x))
    tables.extend([np.cos(twist).astype(np.float32), np.sin(twist).astype(np.float32)])
    return tables


def split(x):
    high = x.astype(bf16)
    return high, (x - high.astype(f32)).astype(bf16)


def mm(a, b):
    return jnp.dot(a, b, preferred_element_type=f32)


def kernel(
    sky_ref, sub_ref, cell_ref, ang_ref, seg_ref, waf_ref, mix_ref, knee_ref,
    f1h, f1l, f2h, f2l, f3h, f3l, f4h, f4l, tc_ref, ts_ref,
    out_ref,
    tab, lhs, iqu, local, cosw, sinw, wts, flat, cs, xb, fs, wb,
    vals, av, oh, acc, r1, s2, r2, s3, r3,
    ag_recv, a1_recv, a2_recv, r1_recv, r2_recv, r3_recv,
    ag_send, a1_send, a2_send, r1_send, r2_send, r3_send,
):
    o = lax.axis_index("obs")
    j = lax.axis_index("dt")
    n_obs = lax.axis_size("obs")
    y, z = j // NZ, j % NZ
    before, after = (o + n_obs - 1) % n_obs, (o + 1) % n_obs

    barrier = pltpu.get_barrier_semaphore()
    for other in (before, after):
        pl.semaphore_signal(barrier, inc=1, device_id={"obs": other}, device_id_type=MESH)

    def greet(k, carry):
        pl.semaphore_signal(barrier, inc=1, device_id={"dt": (j + k) % GROUP}, device_id_type=MESH)
        return carry

    lax.fori_loop(1, GROUP, greet, 0)

    double = 2.0 * ang_ref[0]
    cosw[...] = jnp.cos(double)
    sinw[...] = jnp.sin(double)
    local[...] = (sub_ref[0] - o * GROUP) & (n_obs * GROUP - 1)
    keep = jnp.where((seg_ref[...] & 1) == 0, 1.0, 0.0).astype(f32)
    rows = lax.broadcasted_iota(i32, (256, 128), 0)
    bins = (rows & 127) + 128 * lax.broadcasted_iota(i32, (256, 128), 1)
    freq = jnp.minimum(bins, NSAMP - bins).astype(f32)
    lanes = lax.broadcasted_iota(i32, (1, DET), 1)
    knee = knee_ref[...]
    knee_a = jnp.sum(jnp.where(lanes == 2 * j, knee, 0.0), axis=1, keepdims=True)
    knee_b = jnp.sum(jnp.where(lanes == 2 * j + 1, knee, 0.0), axis=1, keepdims=True)
    knees = jnp.where(rows < 128, knee_a, knee_b)
    square = freq * freq
    wts[...] = square / (square + knees * knees)

    pl.semaphore_wait(barrier, GROUP + 1)

    def sky_copy(src, slot, device):
        return pltpu.make_async_remote_copy(
            src_ref=src, dst_ref=tab.at[slot], send_sem=ag_send, recv_sem=ag_recv.at[slot],
            device_id=device, device_id_type=MESH)

    def arrive(slot):
        sky_copy(sky_ref.at[0], slot, {"obs": before}).wait_recv()

    own = sky_ref.at[0]
    for k in range(1, NZ):
        step = (k + 1) // 2 if k % 2 else NZ - k // 2
        sky_copy(own, j, {"dt": y * NZ + (z + step) % NZ}).start()
    for k in range(1, NY):
        sky_copy(own, j, {"dt": (y + k) % NY * NZ + z}).start()
    sky_copy(own, GROUP + j, {"obs": before}).start()
    tab[pl.ds(j, 1)] = sky_ref[...]
    for k in range(1, NZ):
        step = NZ - (k + 1) // 2 if k % 2 else k // 2
        slot = y * NZ + (z + step) % NZ
        arrive(slot)
        for m in range(1, NY):
            sky_copy(tab.at[slot], slot, {"dt": (y + m) % NY * NZ + z}).start()
        sky_copy(tab.at[slot], GROUP + slot, {"obs": before}).start()

    def pass_on(k, carry):
        turn = k // (NY - 1)
        step = jnp.where(turn % 2 == 0, (NZ - turn // 2) % NZ, (turn + 1) // 2)
        slot = (y + 1 + k % (NY - 1)) % NY * NZ + (z + step) % NZ
        arrive(slot)
        sky_copy(tab.at[slot], GROUP + slot, {"obs": before}).start()
        return carry

    lax.fori_loop(0, NZ * (NY - 1), pass_on, 0)

    def await_next(k, carry):
        arrive(GROUP + k)
        return carry

    lax.fori_loop(0, GROUP, await_next, 0)

    for c in range(3):
        high, low = split(tab[:, c, :])
        lhs[c * WINDOW:(c + 1) * WINDOW, :] = high
        lhs[(3 + c) * WINDOW:(4 + c) * WINDOW, :] = low

    def one_hot(row):
        return jnp.where(lax.broadcasted_iota(i32, (PIX, SPAN), 0) == row, 1.0, 0.0).astype(bf16)

    def gather(g, carry):
        base = pl.multiple_of(g * TILE, TILE)
        cells = cell_ref[0, pl.ds(base, TILE), :]
        subs = local[pl.ds(base, TILE), :]
        found = [[], [], []]
        for i in range(TILE):
            result = mm(lhs[...], one_hot(cells[i:i + 1]))
            mask = lax.broadcasted_iota(i32, (WINDOW, SPAN), 0) == subs[i:i + 1]
            for c in range(3):
                both = result[c * WINDOW:(c + 1) * WINDOW] + result[(3 + c) * WINDOW:(4 + c) * WINDOW]
                found[c].append(jnp.sum(jnp.where(mask, both, 0.0), axis=0, keepdims=True))
        for c in range(3):
            iqu[c, pl.ds(base, TILE), :] = jnp.concatenate(found[c], axis=0)
        return carry

    lax.fori_loop(0, DET // TILE, gather, 0)

    tod = keep * (iqu[0] + cosw[...] * iqu[1] + sinw[...] * iqu[2])
    wafer = jnp.broadcast_to(waf_ref[...], (DET, DET)).astype(f32)
    mixing = jnp.where(wafer.T == wafer, mix_ref[0].astype(f32), 0.0).astype(bf16)
    corr = tod + mm(mixing, tod.astype(bf16))
    for h in range(2):
        flat[h] = corr[:, h * 128:(h + 1) * 128]
        for d in range(2):
            cs[:, 2 * d + h, :] = flat[h, pl.ds(d, GROUP, stride=2), :]

    def exchange(src, dst, send, recv):
        def copy(k):
            other = (j + k) % GROUP
            return pltpu.make_async_remote_copy(
                src_ref=src.at[other], dst_ref=dst.at[j], send_sem=send, recv_sem=recv.at[j],
                device_id={"dt": other}, device_id_type=MESH)

        def push(k, carry):
            copy(k).start()
            return carry

        def take(k, carry):
            other = (j + k) % GROUP
            pltpu.make_async_remote_copy(
                src_ref=src.at[other], dst_ref=dst.at[other], send_sem=send, recv_sem=recv.at[other],
                device_id={"dt": other}, device_id_type=MESH).wait_recv()
            return carry

        lax.fori_loop(1, GROUP, push, 0)
        dst[pl.ds(j, 1)] = src[pl.ds(j, 1)]
        lax.fori_loop(1, GROUP, take, 0)

    exchange(cs, xb, a1_send, a1_recv)

    def exact_left(high, low, x):
        xh, xl = split(x)
        return mm(high[...], xh) + (mm(high[...], xl) + mm(low[...], xh))

    def exact_right(x, high, low):
        xh, xl = split(x)
        return mm(xh, high[...]) + (mm(xl, high[...]) + mm(xh, low[...]))

    series = xb[...].reshape(256, 128)
    part = exact_left(f1h, f1l, series)
    re, im = part[:256], part[256:]
    tc, ts = tc_ref[...], ts_ref[...]
    spec = exact_right(jnp.concatenate([re * tc + im * ts, im * tc - re * ts], axis=1), f2h, f2l)
    weight = wts[...]
    spec = spec * jnp.concatenate([weight, weight], axis=1)
    back = exact_right(spec, f3h, f3l)
    re, im = back[:, :128], back[:, 128:]
    turned = jnp.concatenate([re * tc - im * ts, re * ts + im * tc], axis=0)
    fs[...] = exact_left(f4h, f4l, turned).reshape(GROUP, 4, 128)

    exchange(fs, wb, a2_send, a2_recv)

    for d in range(2):
        for h in range(2):
            flat[h, pl.ds(d, GROUP, stride=2), :] = wb[:, 2 * d + h, :]
    weighted = keep * jnp.concatenate([flat[0], flat[1]], axis=1)
    vals[0] = weighted
    vals[1] = weighted * cosw[...]
    vals[2] = weighted * sinw[...]
    acc[...] = jnp.zeros_like(acc)

    def scatter(g, carry):
        base = pl.multiple_of(g * TILE, TILE)
        cells = cell_ref[0, pl.ds(base, TILE), :]
        subs = local[pl.ds(base, TILE), :]
        value = [vals[c, pl.ds(base, TILE), :] for c in range(3)]
        for i in range(TILE):
            span = slice(i * SPAN, (i + 1) * SPAN)
            oh[:, span] = one_hot(cells[i:i + 1])
            mask = lax.broadcasted_iota(i32, (WINDOW, SPAN), 0) == subs[i:i + 1]
            for c in range(3):
                for t, x in enumerate(split(value[c][i:i + 1])):
                    k = 3 * t + c
                    av[k * WINDOW:(k + 1) * WINDOW, span] = jnp.where(mask, x.astype(f32), 0.0).astype(bf16)
        sums = lax.dot_general(av[...], oh[...], (((1,), (1,)), ((), ())), preferred_element_type=f32)
        for c in range(3):
            acc[c] += sums[c * WINDOW:(c + 1) * WINDOW] + sums[(3 + c) * WINDOW:(4 + c) * WINDOW]
        return carry

    lax.fori_loop(0, DET // TILE, scatter, 0)

    def block(row):
        return acc.at[:, pl.ds(pl.multiple_of(row * NZ, NZ), NZ), :]

    def to_next(row):
        return pltpu.make_async_remote_copy(
            src_ref=block(NY + row), dst_ref=r1.at[row], send_sem=r1_send, recv_sem=r1_recv.at[row],
            device_id={"obs": after}, device_id_type=MESH)

    def to_row(row, slot):
        return pltpu.make_async_remote_copy(
            src_ref=s2.at[row], dst_ref=r2.at[slot], send_sem=r2_send, recv_sem=r2_recv.at[slot],
            device_id={"dt": row * NZ + z}, device_id_type=MESH)

    def to_owner(other, slot):
        return pltpu.make_async_remote_copy(
            src_ref=s3.at[other], dst_ref=r3.at[slot], send_sem=r3_send, recv_sem=r3_recv.at[slot],
            device_id={"dt": y * NZ + other}, device_id_type=MESH)

    turns = [(y + k) % NY for k in (2, 1, 3, 0)]
    for row in turns:
        to_next(row).start()
    for k, row in enumerate(turns):
        to_next(row).wait_recv()
        s2[row] = block(row)[...] + r1[row]
        if k < NY - 1:
            to_row(row, y).start()
    total = s2[y]
    for row in turns[:NY - 1]:
        to_row(row, row).wait_recv()
        total = total + r2[row]
    for k in range(NZ):
        s3[k] = total[:, k, :]
    for k in range(NZ - 1):
        step = NZ // 2 + (k + 1) // 2 if k % 2 == 0 else NZ // 2 - (k + 1) // 2
        to_owner((z + step) % NZ, z).start()
    r3[pl.ds(z, 1)] = s3[pl.ds(z, 1)]
    for k in range(1, NZ):
        other = (z + k) % NZ
        to_owner(other, other).wait_recv()
    result = r3[0]
    for k in range(1, NZ):
        result = result + r3[k]
    out_ref[0] = result

    def sky_sent(k, carry):
        sky_copy(own, j, {"obs": before}).wait_send()
        return carry

    lax.fori_loop(0, (NZ - 1) + (NY - 1) + 1 + (NZ - 1) * NY + NZ * (NY - 1), sky_sent, 0)

    def sent(k, carry):
        for src, dst, send, recv in ((cs, xb, a1_send, a1_recv), (fs, wb, a2_send, a2_recv)):
            pltpu.make_async_remote_copy(
                src_ref=src.at[j], dst_ref=dst.at[j], send_sem=send, recv_sem=recv.at[j],
                device_id={"obs": before}, device_id_type=MESH).wait_send()
        return carry

    lax.fori_loop(1, GROUP, sent, 0)
    for row in range(NY):
        to_next(row).wait_send()
    for k in range(1, NY):
        to_row((y + k) % NY, y).wait_send()
    for k in range(1, NZ):
        to_owner((z + k) % NZ, z).wait_send()


def body(sky_map, submap_of, pixel_cell, angles, intervals, wafer_of, mixing, knee):
    vmem = pl.BlockSpec(memory_space=pltpu.VMEM)
    tables = [jnp.asarray(t) for t in dft_tables()]
    args = [sky_map, submap_of, pixel_cell, angles, intervals, wafer_of, mixing, knee, *tables]
    dma = pltpu.SemaphoreType.DMA
    return pl.pallas_call(
        kernel,
        out_shape=jax.ShapeDtypeStruct((1, 3, PIX), f32),
        in_specs=[vmem] * len(args),
        out_specs=vmem,
        scratch_shapes=[
            pltpu.VMEM((WINDOW, 3, PIX), f32),
            pltpu.VMEM((6 * WINDOW, PIX), bf16),
            pltpu.VMEM((3, DET, SPAN), f32),
            pltpu.VMEM((DET, SPAN), i32),
            pltpu.VMEM((DET, SPAN), f32),
            pltpu.VMEM((DET, SPAN), f32),
            pltpu.VMEM((256, 128), f32),
            pltpu.VMEM((2, DET, 128), f32),
            pltpu.VMEM((GROUP, 4, 128), f32),
            pltpu.VMEM((GROUP, 4, 128), f32),
            pltpu.VMEM((GROUP, 4, 128), f32),
            pltpu.VMEM((GROUP, 4, 128), f32),
            pltpu.VMEM((3, DET, SPAN), f32),
            pltpu.VMEM((6 * WINDOW, TILE * SPAN), bf16),
            pltpu.VMEM((PIX, TILE * SPAN), bf16),
            pltpu.VMEM((3, WINDOW, PIX), f32),
            pltpu.VMEM((NY, 3, NZ, PIX), f32),
            pltpu.VMEM((NY, 3, NZ, PIX), f32),
            pltpu.VMEM((NY, 3, NZ, PIX), f32),
            pltpu.VMEM((NZ, 3, PIX), f32),
            pltpu.VMEM((NZ, 3, PIX), f32),
            dma((WINDOW,)), dma((GROUP,)), dma((GROUP,)), dma((NY,)), dma((NY,)), dma((NZ,)),
            dma, dma, dma, dma, dma, dma,
        ],
        compiler_params=pltpu.CompilerParams(
            collective_id=0, has_side_effects=True, vmem_limit_bytes=60 << 20),
        name="mapmaker",
    )(*args)


def solution(mesh):
    return jax.shard_map(
        body,
        mesh=mesh,
        in_specs=(
            P(("obs", "dt"), None, None),
            P("obs", None, "dt"),
            P("obs", None, "dt"),
            P("obs", None, "dt"),
            P("obs", "dt"),
            P("obs", None),
            P("obs", None, None),
            P("obs", None),
        ),
        out_specs=P(("obs", "dt"), None, None),
        check_vma=False,
    )
```

time: 931 us -> 146 us (0.16)
  waiting for transfers between devices: 303 us -> 0 us
  other arithmetic: 269 us -> 0 us
  local copies, waits for them, and re-layouts: 213 us -> 2.58 us
  Pallas kernels: 0 us -> 142 us
  blocking collectives: 107 us -> 0 us
  starting transfers between devices: 16.3 us -> 0 us
  between operations: 13.8 us -> 0.01 us
    unnamed x2 -> x0, waiting for transfers between devices: 260 us -> none
    scatter-add x1 -> x0, other arithmetic: 187 us -> none  [body(): jnp.zeros((3, patch_pixels), jnp.float32).at[:, local_index.reshape(-1)]]
    pallas_call x0 -> x1, Pallas kernels: none -> 142 us  [body(): pl.pallas_call(kernel, out_shape=jax.ShapeDtypeStruct((1, 3, PIX), f32),...]
    gather x2 -> x0, local copies, waits for them, and re-layouts: 129 us -> none  [body(): sampled = table[:, local_index]]
    all_gather x1 -> x0, blocking collectives: 107 us -> none  [body(): own_patch = lax.all_gather(sky_map, 'dt', axis=0, tiled=True)]
    unnamed x4 -> x0, other arithmetic: 76.9 us -> none
    all_to_all x2 -> x0, waiting for transfers between devices: 31 us -> none  [the longest x1 15.5 us: body(): lax.all_to_all(corr[None], 'dt', split_axis=1, concat_axis=2, tiled=True)]
    unnamed x23 -> x1, local copies, waits for them, and re-layouts: 27.7 us -> 1.29 us
  transfers between devices with their start and end apart: 5 -> 0, of which waited for: 5 -> 0; matrix products, arithmetic and copies ran while one was open for 1% -> 0% of each run, Pallas kernels for 0% -> 0%
where the time goes in v1:
time: 146 us; the launch traced here: 144 us
  Pallas kernels  142 us (97%)
  local copies, waits for them, and re-layouts  2.58 us (2%)
    pallas_call x1, Pallas kernels, body(): pl.pallas_call(kernel, out_shape=jax.ShapeDtypeStruct((1, 3, PIX), f32),...  142 us

profile of v1, /device:TPU:6, one launch (start us, length us, event | category | flops | bytes accessed | tf_op | source)
XLA Modules:
  0.0 144.1 jit_solution(8505385722256731711)
XLA Ops:
  0.0 1.3 copy.19.sky_ref
  1.3 141.5 %mapmaker.1 = f32[1,3,512]{2,1,0:T(4,128)} custom-call(f32[1,3,512]{2,1,0:T(4,128)} %copy.19.sky_ref, s32[1,128,256]{2,1,0:T(8,128)} %sub_ref.1, s32[1,128,256]{2,1,0:T(8,128)} %cell_ref.1, f32[1,128,256]{2,1,0:T(8,128)} %ang_ref.1, s32[1,256]{1,0:T(1,128)} %seg_ref.1, s32[1,128]{1,0:T(1,128)} %waf_ref.1, bf16[1,128,128]{2,1,0:T(8,128)(2,1)} %mix_ref.1, ...), custom_call_target="tpu_custom_call" | custom-call | tf_op jit(solution)/shard_map/mapmaker/pallas_call | solution.py:326
  142.8 1.3 copy.20

commit v2 on v1

--- a/solution.py
+++ b/solution.py
@@ -17,6 +17,7 @@
 PIX = 512
 GROUP = 64
 NY, NZ = 4, 16
+REACH = 4
 WINDOW = 2 * GROUP
 NSAMP = GROUP * SPAN
 TILE = 8
@@ -31,7 +32,7 @@
 def dft_tables():
     n = 128
     row = np.arange(256)
-    row_det, row_n1 = (row // 2) % 2, 2 * (row // 4) + row % 2
+    row_det, row_n1 = row % 2, 2 * ((row % n) // 2) + row // n
     col_det, col_k1 = row // n, row % n
     same = (row_det[:, None] == col_det[None, :]).astype(np.float64)
     turn = 2.0 * np.pi * ((row_n1[:, None] * col_k1[None, :]) % n) / n
@@ -64,26 +65,26 @@
     sky_ref, sub_ref, cell_ref, ang_ref, seg_ref, waf_ref, mix_ref, knee_ref,
     f1h, f1l, f2h, f2l, f3h, f3l, f4h, f4l, tc_ref, ts_ref,
     out_ref,
-    tab, lhs, iqu, local, cosw, sinw, wts, flat, cs, xb, fs, wb,
-    vals, av, oh, acc, r1, s2, r2, s3, r3,
+    tab, lhs, iqu, local, cosw, sinw, wts, cs, xb, fs, wb,
+    av, oh, acc, r1, s2, r2, s3, r3,
     ag_recv, a1_recv, a2_recv, r1_recv, r2_recv, r3_recv,
     ag_send, a1_send, a2_send, r1_send, r2_send, r3_send,
 ):
     o = lax.axis_index("obs")
     j = lax.axis_index("dt")
     n_obs = lax.axis_size("obs")
-    y, z = j // NZ, j % NZ
-    before, after = (o + n_obs - 1) % n_obs, (o + 1) % n_obs
+    y, z = j >> 4, j & (NZ - 1)
+    before, after = (o + n_obs - 1) & (n_obs - 1), (o + 1) & (n_obs - 1)
+
+    def chip(dy, dz):
+        return ((y + dy) & (NY - 1)) * NZ + ((z + dz) & (NZ - 1))
 
     barrier = pltpu.get_barrier_semaphore()
+    near = [chip(0, s) for s in range(-REACH, REACH + 1) if s] + [chip(s, 0) for s in range(1, NY)]
+    for other in near:
+        pl.semaphore_signal(barrier, inc=1, device_id={"dt": other}, device_id_type=MESH)
     for other in (before, after):
         pl.semaphore_signal(barrier, inc=1, device_id={"obs": other}, device_id_type=MESH)
-
-    def greet(k, carry):
-        pl.semaphore_signal(barrier, inc=1, device_id={"dt": (j + k) % GROUP}, device_id_type=MESH)
-        return carry
-
-    lax.fori_loop(1, GROUP, greet, 0)
 
     double = 2.0 * ang_ref[0]
     cosw[...] = jnp.cos(double)
@@ -101,41 +102,69 @@
     square = freq * freq
     wts[...] = square / (square + knees * knees)
 
-    pl.semaphore_wait(barrier, GROUP + 1)
+    pl.semaphore_wait(barrier, len(near) + 2)
 
     def sky_copy(src, slot, device):
         return pltpu.make_async_remote_copy(
             src_ref=src, dst_ref=tab.at[slot], send_sem=ag_send, recv_sem=ag_recv.at[slot],
             device_id=device, device_id_type=MESH)
 
+    own = sky_ref
+
+    def send(slot, device):
+        sky_copy(tab.at[slot], slot, device).start()
+
+    def to_before(slot):
+        sky_copy(tab.at[slot], GROUP + slot, {"obs": before}).start()
+
     def arrive(slot):
-        sky_copy(sky_ref.at[0], slot, {"obs": before}).wait_recv()
-
-    own = sky_ref.at[0]
-    for k in range(1, NZ):
-        step = (k + 1) // 2 if k % 2 else NZ - k // 2
-        sky_copy(own, j, {"dt": y * NZ + (z + step) % NZ}).start()
-    for k in range(1, NY):
-        sky_copy(own, j, {"dt": (y + k) % NY * NZ + z}).start()
+        sky_copy(own, slot, {"obs": before}).wait_recv()
+
+    for s in range(REACH, 0, -1):
+        for step in (s, -s):
+            sky_copy(own, j, {"dt": chip(0, step)}).start()
+    for step in (1, -1):
+        sky_copy(own, j, {"dt": chip(step, 0)}).start()
     sky_copy(own, GROUP + j, {"obs": before}).start()
-    tab[pl.ds(j, 1)] = sky_ref[...]
-    for k in range(1, NZ):
-        step = NZ - (k + 1) // 2 if k % 2 else k // 2
-        slot = y * NZ + (z + step) % NZ
+    tab[pl.ds(j, 1)] = sky_ref[...][None]
+    sky_sends = 2 * REACH + 3
+    for s in range(1, NZ // 2 + 1):
+        for sign in (1, -1) if s < NZ // 2 else (1,):
+            slot = chip(0, -sign * s)
+            arrive(slot)
+            if s == REACH:
+                for far in range(REACH if sign == 1 else REACH - 1, 0, -1):
+                    send(slot, {"dt": chip(0, sign * far)})
+                    sky_sends += 1
+            send(slot, {"dt": chip(1, 0)})
+            send(slot, {"dt": chip(-1, 0)})
+            to_before(slot)
+            sky_sends += 3
+
+    def offset(k):
+        return jnp.where((k & 1) == 1, -((k + 1) >> 1), k >> 1)
+
+    def pass_on(k, carry):
+        dz = offset(k)
+        odd = (z + dz) & 1
+        low, high = chip(-1, dz), chip(1, dz)
+        arrive(low)
+        arrive(high)
+        send(chip(2 * odd - 1, dz), {"dt": chip(1 - 2 * odd, 0)})
+        to_before(low)
+        to_before(high)
+        return carry
+
+    lax.fori_loop(0, NZ, pass_on, 0)
+
+    def pass_last(k, carry):
+        slot = chip(2, offset(k))
         arrive(slot)
-        for m in range(1, NY):
-            sky_copy(tab.at[slot], slot, {"dt": (y + m) % NY * NZ + z}).start()
-        sky_copy(tab.at[slot], GROUP + slot, {"obs": before}).start()
-
-    def pass_on(k, carry):
-        turn = k // (NY - 1)
-        step = jnp.where(turn % 2 == 0, (NZ - turn // 2) % NZ, (turn + 1) // 2)
-        slot = (y + 1 + k % (NY - 1)) % NY * NZ + (z + step) % NZ
-        arrive(slot)
-        sky_copy(tab.at[slot], GROUP + slot, {"obs": before}).start()
-        return carry
-
-    lax.fori_loop(0, NZ * (NY - 1), pass_on, 0)
+        to_before(slot)
+        return carry
+
+    lax.fori_loop(0, NZ, pass_last, 0)
+    sky_sends += 4 * NZ
 
     def await_next(k, carry):
         arrive(GROUP + k)
@@ -144,7 +173,7 @@
     lax.fori_loop(0, GROUP, await_next, 0)
 
     for c in range(3):
-        high, low = split(tab[:, c, :])
+        high, low = split(tab[:, c, 0, :])
         lhs[c * WINDOW:(c + 1) * WINDOW, :] = high
         lhs[(3 + c) * WINDOW:(4 + c) * WINDOW, :] = low
 
@@ -172,34 +201,33 @@
     wafer = jnp.broadcast_to(waf_ref[...], (DET, DET)).astype(f32)
     mixing = jnp.where(wafer.T == wafer, mix_ref[0].astype(f32), 0.0).astype(bf16)
     corr = tod + mm(mixing, tod.astype(bf16))
-    for h in range(2):
-        flat[h] = corr[:, h * 128:(h + 1) * 128]
-        for d in range(2):
-            cs[:, 2 * d + h, :] = flat[h, pl.ds(d, GROUP, stride=2), :]
-
-    def exchange(src, dst, send, recv):
-        def copy(k):
-            other = (j + k) % GROUP
-            return pltpu.make_async_remote_copy(
-                src_ref=src.at[other], dst_ref=dst.at[j], send_sem=send, recv_sem=recv.at[j],
-                device_id={"dt": other}, device_id_type=MESH)
-
+    for i in range(GROUP):
+        cs[i] = corr[2 * i:2 * i + 2]
+
+    def piece(src, dst, send_sem, recv_sem, here, there, device):
+        return pltpu.make_async_remote_copy(
+            src_ref=src.at[here], dst_ref=dst.at[there], send_sem=send_sem, recv_sem=recv_sem.at[there],
+            device_id={"dt": device}, device_id_type=MESH)
+
+    def spread(src, dst, send_sem, recv_sem):
         def push(k, carry):
-            copy(k).start()
-            return carry
-
-        def take(k, carry):
-            other = (j + k) % GROUP
-            pltpu.make_async_remote_copy(
-                src_ref=src.at[other], dst_ref=dst.at[other], send_sem=send, recv_sem=recv.at[other],
-                device_id={"dt": other}, device_id_type=MESH).wait_recv()
+            other = (j + k) & (GROUP - 1)
+            piece(src, dst, send_sem, recv_sem, other, j, other).start()
             return carry
 
         lax.fori_loop(1, GROUP, push, 0)
         dst[pl.ds(j, 1)] = src[pl.ds(j, 1)]
-        lax.fori_loop(1, GROUP, take, 0)
-
-    exchange(cs, xb, a1_send, a1_recv)
+
+    def take(src, dst, send_sem, recv_sem, source):
+        piece(src, dst, send_sem, recv_sem, source, source, source).wait_recv()
+
+    spread(cs, xb, a1_send, a1_recv)
+
+    def take_series(k, carry):
+        take(cs, xb, a1_send, a1_recv, (j + k) & (GROUP - 1))
+        return carry
+
+    lax.fori_loop(1, GROUP, take_series, 0)
 
     def exact_left(high, low, x):
         xh, xl = split(x)
@@ -209,7 +237,8 @@
         xh, xl = split(x)
         return mm(xh, high[...]) + (mm(xl, high[...]) + mm(xh, low[...]))
 
-    series = xb[...].reshape(256, 128)
+    pairs = jnp.concatenate([xb[i] for i in range(GROUP)], axis=0)
+    series = jnp.concatenate([pairs[:, :128], pairs[:, 128:]], axis=0)
     part = exact_left(f1h, f1l, series)
     re, im = part[:256], part[256:]
     tc, ts = tc_ref[...], ts_ref[...]
@@ -219,24 +248,29 @@
     back = exact_right(spec, f3h, f3l)
     re, im = back[:, :128], back[:, 128:]
     turned = jnp.concatenate([re * tc - im * ts, re * ts + im * tc], axis=0)
-    fs[...] = exact_left(f4h, f4l, turned).reshape(GROUP, 4, 128)
-
-    exchange(fs, wb, a2_send, a2_recv)
-
-    for d in range(2):
-        for h in range(2):
-            flat[h, pl.ds(d, GROUP, stride=2), :] = wb[:, 2 * d + h, :]
-    weighted = keep * jnp.concatenate([flat[0], flat[1]], axis=1)
-    vals[0] = weighted
-    vals[1] = weighted * cosw[...]
-    vals[2] = weighted * sinw[...]
+    filtered = exact_left(f4h, f4l, turned)
+    filtered = jnp.concatenate([filtered[:128], filtered[128:]], axis=1)
+    for i in range(GROUP):
+        fs[i] = filtered[2 * i:2 * i + 2]
+    spread(fs, wb, a2_send, a2_recv)
+
     acc[...] = jnp.zeros_like(acc)
 
-    def scatter(g, carry):
+    def scatter(k, carry):
+        dq = k >> 2
+        g = ((y + k) & (NY - 1)) * 4 + (((z >> 2) + jnp.where(dq >= 2, 5 - dq, dq)) & 3)
+        for i in range(TILE // 2):
+            source = g * (TILE // 2) + i
+
+            @pl.when(source != j)
+            def _():
+                take(fs, wb, a2_send, a2_recv, source)
+
         base = pl.multiple_of(g * TILE, TILE)
         cells = cell_ref[0, pl.ds(base, TILE), :]
         subs = local[pl.ds(base, TILE), :]
-        value = [vals[c, pl.ds(base, TILE), :] for c in range(3)]
+        weighted = jnp.concatenate([wb[g * (TILE // 2) + i] for i in range(TILE // 2)], axis=0) * keep
+        value = [weighted, weighted * cosw[pl.ds(base, TILE), :], weighted * sinw[pl.ds(base, TILE), :]]
         for i in range(TILE):
             span = slice(i * SPAN, (i + 1) * SPAN)
             oh[:, span] = one_hot(cells[i:i + 1])
@@ -270,7 +304,7 @@
             src_ref=s3.at[other], dst_ref=r3.at[slot], send_sem=r3_send, recv_sem=r3_recv.at[slot],
             device_id={"dt": y * NZ + other}, device_id_type=MESH)
 
-    turns = [(y + k) % NY for k in (2, 1, 3, 0)]
+    turns = [(y + k) & (NY - 1) for k in (2, 1, 3, 0)]
     for row in turns:
         to_next(row).start()
     for k, row in enumerate(turns):
@@ -286,21 +320,21 @@
         s3[k] = total[:, k, :]
     for k in range(NZ - 1):
         step = NZ // 2 + (k + 1) // 2 if k % 2 == 0 else NZ // 2 - (k + 1) // 2
-        to_owner((z + step) % NZ, z).start()
+        to_owner((z + step) & (NZ - 1), z).start()
     r3[pl.ds(z, 1)] = s3[pl.ds(z, 1)]
     for k in range(1, NZ):
-        other = (z + k) % NZ
+        other = (z + k) & (NZ - 1)
         to_owner(other, other).wait_recv()
     result = r3[0]
     for k in range(1, NZ):
         result = result + r3[k]
-    out_ref[0] = result
+    out_ref[...] = result[:, None, :]
 
     def sky_sent(k, carry):
         sky_copy(own, j, {"obs": before}).wait_send()
         return carry
 
-    lax.fori_loop(0, (NZ - 1) + (NY - 1) + 1 + (NZ - 1) * NY + NZ * (NY - 1), sky_sent, 0)
+    lax.fori_loop(0, sky_sends, sky_sent, 0)
 
     def sent(k, carry):
         for src, dst, send, recv in ((cs, xb, a1_send, a1_recv), (fs, wb, a2_send, a2_recv)):
@@ -313,35 +347,33 @@
     for row in range(NY):
         to_next(row).wait_send()
     for k in range(1, NY):
-        to_row((y + k) % NY, y).wait_send()
+        to_row((y + k) & (NY - 1), y).wait_send()
     for k in range(1, NZ):
-        to_owner((z + k) % NZ, z).wait_send()
+        to_owner((z + k) & (NZ - 1), z).wait_send()
 
 
 def body(sky_map, submap_of, pixel_cell, angles, intervals, wafer_of, mixing, knee):
     vmem = pl.BlockSpec(memory_space=pltpu.VMEM)
     tables = [jnp.asarray(t) for t in dft_tables()]
-    args = [sky_map, submap_of, pixel_cell, angles, intervals, wafer_of, mixing, knee, *tables]
+    args = [jnp.transpose(sky_map, (1, 0, 2)), submap_of, pixel_cell, angles, intervals, wafer_of, mixing, knee, *tables]
     dma = pltpu.SemaphoreType.DMA
-    return pl.pallas_call(
+    result = pl.pallas_call(
         kernel,
-        out_shape=jax.ShapeDtypeStruct((1, 3, PIX), f32),
+        out_shape=jax.ShapeDtypeStruct((3, 1, PIX), f32),
         in_specs=[vmem] * len(args),
         out_specs=vmem,
         scratch_shapes=[
-            pltpu.VMEM((WINDOW, 3, PIX), f32),
+            pltpu.VMEM((WINDOW, 3, 1, PIX), f32),
             pltpu.VMEM((6 * WINDOW, PIX), bf16),
             pltpu.VMEM((3, DET, SPAN), f32),
             pltpu.VMEM((DET, SPAN), i32),
             pltpu.VMEM((DET, SPAN), f32),
             pltpu.VMEM((DET, SPAN), f32),
             pltpu.VMEM((256, 128), f32),
-            pltpu.VMEM((2, DET, 128), f32),
-            pltpu.VMEM((GROUP, 4, 128), f32),
-            pltpu.VMEM((GROUP, 4, 128), f32),
-            pltpu.VMEM((GROUP, 4, 128), f32),
-            pltpu.VMEM((GROUP, 4, 128), f32),
-            pltpu.VMEM((3, DET, SPAN), f32),
+            pltpu.VMEM((GROUP, 2, SPAN), f32),
+            pltpu.VMEM((GROUP, 2, SPAN), f32),
+            pltpu.VMEM((GROUP, 2, SPAN), f32),
+            pltpu.VMEM((GROUP, 2, SPAN), f32),
             pltpu.VMEM((6 * WINDOW, TILE * SPAN), bf16),
             pltpu.VMEM((PIX, TILE * SPAN), bf16),
             pltpu.VMEM((3, WINDOW, PIX), f32),
@@ -357,6 +389,7 @@
             collective_id=0, has_side_effects=True, vmem_limit_bytes=60 << 20),
         name="mapmaker",
     )(*args)
+    return jnp.transpose(result, (1, 0, 2))
 
 
 def solution(mesh):

time: 146 us -> 135 us (0.925)
  Pallas kernels: 142 us -> 132 us
    pallas_call x1, Pallas kernels: 142 us -> 132 us  [body(): pl.pallas_call(kernel, out_shape=jax.ShapeDtypeStruct((3, 1, PIX), f32),...]
where the time goes in v2:
time: 135 us; the launch traced here: 133 us
  Pallas kernels  132 us (98%)
    pallas_call x1, Pallas kernels, body(): pl.pallas_call(kernel, out_shape=jax.ShapeDtypeStruct((3, 1, PIX), f32),...  132 us

profile of v2, /device:TPU:6, one launch (start us, length us, event | category | flops | bytes accessed | tf_op | source)
XLA Modules:
  0.0 132.9 jit_solution(14037389219852340385)
XLA Ops:
  0.0 131.7 %mapmaker.1 = f32[3,1,512]{2,1,0:T(1,128)} custom-call(f32[3,1,512]{2,1,0:T(1,128)} %bitcast.3, s32[1,128,256]{2,1,0:T(8,128)} %sub_ref.1, s32[1,128,256]{2,1,0:T(8,128)} %cell_ref.1, f32[1,128,256]{2,1,0:T(8,128)} %ang_ref.1, s32[1,256]{1,0:T(1,128)} %seg_ref.1, s32[1,128]{1,0:T(1,128)} %waf_ref.1, bf16[1,128,128]{2,1,0:T(8,128)(2,1)} %mix_ref.1, ...), custom_call_target="tpu_custom_call" | custom-call | tf_op jit(solution)/shard_map/mapmaker/pallas_call | solution.py:360
  131.7 1.3 copy.20

commit v3 on v2

--- a/solution.py
+++ b/solution.py
@@ -18,6 +18,7 @@
 GROUP = 64
 NY, NZ = 4, 16
 REACH = 4
+LAG = 3
 WINDOW = 2 * GROUP
 NSAMP = GROUP * SPAN
 TILE = 8
@@ -61,15 +62,24 @@
     return jnp.dot(a, b, preferred_element_type=f32)
 
 
-def kernel(
-    sky_ref, sub_ref, cell_ref, ang_ref, seg_ref, waf_ref, mix_ref, knee_ref,
-    f1h, f1l, f2h, f2l, f3h, f3l, f4h, f4l, tc_ref, ts_ref,
-    out_ref,
-    tab, lhs, iqu, local, cosw, sinw, wts, cs, xb, fs, wb,
-    av, oh, acc, r1, s2, r2, s3, r3,
-    ag_recv, a1_recv, a2_recv, r1_recv, r2_recv, r3_recv,
-    ag_send, a1_send, a2_send, r1_send, r2_send, r3_send,
-):
+INPUTS = 17
+
+
+def kernel(sky_ref, *refs):
+    held, refs = refs[:INPUTS], refs[INPUTS:]
+    out_ref, refs = refs[0], refs[1:]
+    local_copies, refs = refs[:INPUTS], refs[INPUTS:]
+    (
+        sub_ref, cell_ref, ang_ref, seg_ref, waf_ref, mix_ref, knee_ref,
+        f1h, f1l, f2h, f2l, f3h, f3l, f4h, f4l, tc_ref, ts_ref,
+    ) = local_copies
+    (
+        in_sem,
+        tab, lhs, iqu, local, cosw, sinw, wts, cs, xb, fs, wb,
+        av, oh, acc, r1, s2, r2, s3, r3,
+        ag_recv, a1_recv, a2_recv, r1_recv, r2_recv, r3_recv,
+        ag_send, a1_send, a2_send, r1_send, r2_send, r3_send,
+    ) = refs
     o = lax.axis_index("obs")
     j = lax.axis_index("dt")
     n_obs = lax.axis_size("obs")
@@ -85,6 +95,18 @@
         pl.semaphore_signal(barrier, inc=1, device_id={"dt": other}, device_id_type=MESH)
     for other in (before, after):
         pl.semaphore_signal(barrier, inc=1, device_id={"obs": other}, device_id_type=MESH)
+
+    def load(k):
+        return pltpu.make_async_copy(held[k], local_copies[k], in_sem.at[k])
+
+    own_block = pltpu.make_async_copy(sky_ref, tab.at[j], in_sem.at[INPUTS])
+    early, late = (2, 0, 3, 6), (1, 4, 5, *range(7, INPUTS))
+    for k in (*early, *late):
+        load(k).start()
+    own_block.start()
+    acc[...] = jnp.zeros_like(acc)
+    for k in early:
+        load(k).wait()
 
     double = 2.0 * ang_ref[0]
     cosw[...] = jnp.cos(double)
@@ -123,48 +145,48 @@
     for s in range(REACH, 0, -1):
         for step in (s, -s):
             sky_copy(own, j, {"dt": chip(0, step)}).start()
-    for step in (1, -1):
+    for step in (2, 1, -1):
         sky_copy(own, j, {"dt": chip(step, 0)}).start()
     sky_copy(own, GROUP + j, {"obs": before}).start()
-    tab[pl.ds(j, 1)] = sky_ref[...][None]
-    sky_sends = 2 * REACH + 3
+    sky_sends = 2 * REACH + NY
+
+    def signs(s):
+        return (1, -1) if 0 < s < NZ // 2 else (1,)
+
+    def from_rows(s):
+        for sign in signs(s):
+            for dy in (1, -1, 2):
+                slot = chip(dy, -sign * s)
+                arrive(slot)
+                to_before(slot)
+
     for s in range(1, NZ // 2 + 1):
-        for sign in (1, -1) if s < NZ // 2 else (1,):
+        for sign in signs(s):
             slot = chip(0, -sign * s)
             arrive(slot)
             if s == REACH:
                 for far in range(REACH if sign == 1 else REACH - 1, 0, -1):
                     send(slot, {"dt": chip(0, sign * far)})
                     sky_sends += 1
-            send(slot, {"dt": chip(1, 0)})
-            send(slot, {"dt": chip(-1, 0)})
+            for dy in (2, 1, -1):
+                send(slot, {"dt": chip(dy, 0)})
             to_before(slot)
-            sky_sends += 3
-
-    def offset(k):
-        return jnp.where((k & 1) == 1, -((k + 1) >> 1), k >> 1)
-
-    def pass_on(k, carry):
-        dz = offset(k)
-        odd = (z + dz) & 1
-        low, high = chip(-1, dz), chip(1, dz)
-        arrive(low)
-        arrive(high)
-        send(chip(2 * odd - 1, dz), {"dt": chip(1 - 2 * odd, 0)})
-        to_before(low)
-        to_before(high)
-        return carry
-
-    lax.fori_loop(0, NZ, pass_on, 0)
-
-    def pass_last(k, carry):
-        slot = chip(2, offset(k))
-        arrive(slot)
-        to_before(slot)
-        return carry
-
-    lax.fori_loop(0, NZ, pass_last, 0)
-    sky_sends += 4 * NZ
+            sky_sends += NY
+        if s >= LAG:
+            from_rows(s - LAG)
+    for s in range(NZ // 2 + 1 - LAG, NZ // 2 + 1):
+        from_rows(s)
+    sky_sends += NZ * (NY - 1)
+
+    def prepare(first):
+        for c in range(3):
+            high, low = split(tab[first:first + GROUP, c, 0, :])
+            row = c * WINDOW + first
+            lhs[row:row + GROUP, :] = high
+            lhs[3 * WINDOW + row:3 * WINDOW + row + GROUP, :] = low
+
+    own_block.wait()
+    prepare(0)
 
     def await_next(k, carry):
         arrive(GROUP + k)
@@ -172,10 +194,9 @@
 
     lax.fori_loop(0, GROUP, await_next, 0)
 
-    for c in range(3):
-        high, low = split(tab[:, c, 0, :])
-        lhs[c * WINDOW:(c + 1) * WINDOW, :] = high
-        lhs[(3 + c) * WINDOW:(4 + c) * WINDOW, :] = low
+    prepare(GROUP)
+    for k in late:
+        load(k).wait()
 
     def one_hot(row):
         return jnp.where(lax.broadcasted_iota(i32, (PIX, SPAN), 0) == row, 1.0, 0.0).astype(bf16)
@@ -221,7 +242,20 @@
     def take(src, dst, send_sem, recv_sem, source):
         piece(src, dst, send_sem, recv_sem, source, source, source).wait_recv()
 
+    def all_left(src, send_sem, dst, recv_sem):
+        def left(k, carry):
+            piece(src, dst, send_sem, recv_sem, j, j, (j + 1) & (GROUP - 1)).wait_send()
+            return carry
+
+        lax.fori_loop(1, GROUP, left, 0)
+
     spread(cs, xb, a1_send, a1_recv)
+
+    def sky_left(k, carry):
+        sky_copy(own, j, {"obs": before}).wait_send()
+        return carry
+
+    lax.fori_loop(0, sky_sends, sky_left, 0)
 
     def take_series(k, carry):
         take(cs, xb, a1_send, a1_recv, (j + k) & (GROUP - 1))
@@ -253,8 +287,7 @@
     for i in range(GROUP):
         fs[i] = filtered[2 * i:2 * i + 2]
     spread(fs, wb, a2_send, a2_recv)
-
-    acc[...] = jnp.zeros_like(acc)
+    all_left(cs, a1_send, xb, a1_recv)
 
     def scatter(k, carry):
         dq = k >> 2
@@ -286,18 +319,22 @@
 
     lax.fori_loop(0, DET // TILE, scatter, 0)
 
-    def block(row):
-        return acc.at[:, pl.ds(pl.multiple_of(row * NZ, NZ), NZ), :]
-
-    def to_next(row):
+    half = NZ // 2
+    far_half = 1 - (z >> 3)
+    halves = (far_half, 1 - far_half)
+
+    def block(row, part):
+        return acc.at[:, pl.ds(pl.multiple_of(row * NZ + part * half, half), half), :]
+
+    def to_next(row, part):
         return pltpu.make_async_remote_copy(
-            src_ref=block(NY + row), dst_ref=r1.at[row], send_sem=r1_send, recv_sem=r1_recv.at[row],
-            device_id={"obs": after}, device_id_type=MESH)
-
-    def to_row(row, slot):
+            src_ref=block(NY + row, part), dst_ref=r1.at[part, row], send_sem=r1_send,
+            recv_sem=r1_recv.at[part, row], device_id={"obs": after}, device_id_type=MESH)
+
+    def to_row(row, part, slot):
         return pltpu.make_async_remote_copy(
-            src_ref=s2.at[row], dst_ref=r2.at[slot], send_sem=r2_send, recv_sem=r2_recv.at[slot],
-            device_id={"dt": row * NZ + z}, device_id_type=MESH)
+            src_ref=s2.at[part, row], dst_ref=r2.at[part, slot], send_sem=r2_send,
+            recv_sem=r2_recv.at[part, slot], device_id={"dt": row * NZ + z}, device_id_type=MESH)
 
     def to_owner(other, slot):
         return pltpu.make_async_remote_copy(
@@ -305,22 +342,28 @@
             device_id={"dt": y * NZ + other}, device_id_type=MESH)
 
     turns = [(y + k) & (NY - 1) for k in (2, 1, 3, 0)]
-    for row in turns:
-        to_next(row).start()
-    for k, row in enumerate(turns):
-        to_next(row).wait_recv()
-        s2[row] = block(row)[...] + r1[row]
-        if k < NY - 1:
-            to_row(row, y).start()
-    total = s2[y]
-    for row in turns[:NY - 1]:
-        to_row(row, row).wait_recv()
-        total = total + r2[row]
-    for k in range(NZ):
-        s3[k] = total[:, k, :]
-    for k in range(NZ - 1):
-        step = NZ // 2 + (k + 1) // 2 if k % 2 == 0 else NZ // 2 - (k + 1) // 2
-        to_owner((z + step) & (NZ - 1), z).start()
+    for part in halves:
+        for row in turns:
+            to_next(row, part).start()
+    for part in halves:
+        for k, row in enumerate(turns):
+            to_next(row, part).wait_recv()
+            s2[part, row] = block(row, part)[...] + r1[part, row]
+            if k < NY - 1:
+                to_row(row, part, y).start()
+    for part in halves:
+        total = s2[part, y]
+        for row in turns[:NY - 1]:
+            to_row(row, part, row).wait_recv()
+            total = total + r2[part, row]
+        for k in range(half):
+            other = part * half + k
+            s3[other] = total[:, k, :]
+
+            @pl.when(other != z)
+            def _():
+                to_owner(other, z).start()
+
     r3[pl.ds(z, 1)] = s3[pl.ds(z, 1)]
     for k in range(1, NZ):
         other = (z + k) & (NZ - 1)
@@ -330,24 +373,12 @@
         result = result + r3[k]
     out_ref[...] = result[:, None, :]
 
-    def sky_sent(k, carry):
-        sky_copy(own, j, {"obs": before}).wait_send()
-        return carry
-
-    lax.fori_loop(0, sky_sends, sky_sent, 0)
-
-    def sent(k, carry):
-        for src, dst, send, recv in ((cs, xb, a1_send, a1_recv), (fs, wb, a2_send, a2_recv)):
-            pltpu.make_async_remote_copy(
-                src_ref=src.at[j], dst_ref=dst.at[j], send_sem=send, recv_sem=recv.at[j],
-                device_id={"obs": before}, device_id_type=MESH).wait_send()
-        return carry
-
-    lax.fori_loop(1, GROUP, sent, 0)
-    for row in range(NY):
-        to_next(row).wait_send()
-    for k in range(1, NY):
-        to_row((y + k) & (NY - 1), y).wait_send()
+    all_left(fs, a2_send, wb, a2_recv)
+    for part in range(2):
+        for row in range(NY):
+            to_next(row, part).wait_send()
+        for k in range(1, NY):
+            to_row((y + k) & (NY - 1), part, y).wait_send()
     for k in range(1, NZ):
         to_owner((z + k) & (NZ - 1), z).wait_send()
 
@@ -360,9 +391,11 @@
     result = pl.pallas_call(
         kernel,
         out_shape=jax.ShapeDtypeStruct((3, 1, PIX), f32),
-        in_specs=[vmem] * len(args),
+        in_specs=[pl.BlockSpec(memory_space=pl.ANY)] * len(args),
         out_specs=vmem,
         scratch_shapes=[
+            *[pltpu.VMEM(a.shape, a.dtype) for a in args[1:]],
+            dma((INPUTS + 1,)),
             pltpu.VMEM((WINDOW, 3, 1, PIX), f32),
             pltpu.VMEM((6 * WINDOW, PIX), bf16),
             pltpu.VMEM((3, DET, SPAN), f32),
@@ -377,12 +410,12 @@
             pltpu.VMEM((6 * WINDOW, TILE * SPAN), bf16),
             pltpu.VMEM((PIX, TILE * SPAN), bf16),
             pltpu.VMEM((3, WINDOW, PIX), f32),
-            pltpu.VMEM((NY, 3, NZ, PIX), f32),
-            pltpu.VMEM((NY, 3, NZ, PIX), f32),
-            pltpu.VMEM((NY, 3, NZ, PIX), f32),
+            pltpu.VMEM((2, NY, 3, NZ // 2, PIX), f32),
+            pltpu.VMEM((2, NY, 3, NZ // 2, PIX), f32),
+            pltpu.VMEM((2, NY, 3, NZ // 2, PIX), f32),
             pltpu.VMEM((NZ, 3, PIX), f32),
             pltpu.VMEM((NZ, 3, PIX), f32),
-            dma((WINDOW,)), dma((GROUP,)), dma((GROUP,)), dma((NY,)), dma((NY,)), dma((NZ,)),
+            dma((WINDOW,)), dma((GROUP,)), dma((GROUP,)), dma((2, NY)), dma((2, NY)), dma((NZ,)),
             dma, dma, dma, dma, dma, dma,
         ],
         compiler_params=pltpu.CompilerParams(

time: 135 us -> 128 us (0.948); the launches traced: 133 us -> 128 us
  Pallas kernels: 132 us -> 127 us
    pallas_call x1, Pallas kernels: 132 us -> 127 us  [body(): pl.pallas_call(kernel, out_shape=jax.ShapeDtypeStruct((3, 1, PIX), f32),...]
where the time goes in v3:
time: 128 us
  Pallas kernels  127 us (99%)
  local copies, waits for them, and re-layouts  1.29 us (1%)
    pallas_call x1, Pallas kernels, body(): pl.pallas_call(kernel, out_shape=jax.ShapeDtypeStruct((3, 1, PIX), f32),...  127 us

profile of v3, /device:TPU:6, one launch (start us, length us, event | category | flops | bytes accessed | tf_op | source)
XLA Modules:
  0.0 127.9 jit_solution(14343903890489423481)
XLA Ops:
  0.0 126.6 %mapmaker.1 = f32[3,1,512]{2,1,0:T(1,128)} custom-call(f32[3,1,512]{2,1,0:T(1,128)} %bitcast.3, s32[1,128,256]{2,1,0:T(8,128)} %refs_0_.1, s32[1,128,256]{2,1,0:T(8,128)} %refs_1_.1, f32[1,128,256]{2,1,0:T(8,128)} %refs_2_.1, s32[1,256]{1,0:T(1,128)} %refs_3_.1, s32[1,128]{1,0:T(1,128)} %refs_4_.1, bf16[1,128,128]{2,1,0:T(8,128)(2,1)} %refs_5_.1, ...), custom_call_target="tpu_custom_call" | custom-call | tf_op jit(solution)/shard_map/mapmaker/pallas_call | solution.py:391
  126.6 1.3 %copy.20 = f32[1,3,512]{2,0,1:T(1,128)} copy(f32[1,3,512]{2,0,1:T(1,128)} %bitcast.2) | data formatting | bytes 12288

commit v4 on v3

--- a/solution.py
+++ b/solution.py
@@ -76,15 +76,19 @@
     (
         in_sem,
         tab, lhs, iqu, local, cosw, sinw, wts, cs, xb, fs, wb,
-        av, oh, acc, r1, s2, r2, s3, r3,
-        ag_recv, a1_recv, a2_recv, r1_recv, r2_recv, r3_recv,
-        ag_send, a1_send, a2_send, r1_send, r2_send, r3_send,
+        av, oh, acc, r1, s2, r2, r4, s3, r3,
+        ag_recv, a1_recv, a2_recv, r1_recv, r2_recv, r4_recv, r3_recv,
+        ag_send, a1_send, a2_send, r1_send, r2_send, r4_send, r3_send,
     ) = refs
     o = lax.axis_index("obs")
     j = lax.axis_index("dt")
     n_obs = lax.axis_size("obs")
     y, z = j >> 4, j & (NZ - 1)
     before, after = (o + n_obs - 1) & (n_obs - 1), (o + 1) & (n_obs - 1)
+
+    offsets = sorted(
+        ((dy, dz) for dy in range(-1, NY - 1) for dz in range(1 - NZ // 2, NZ // 2 + 1) if dy or dz),
+        key=lambda p: abs(p[0]) + abs(p[1]))
 
     def chip(dy, dz):
         return ((y + dy) & (NY - 1)) * NZ + ((z + dz) & (NZ - 1))
@@ -188,11 +192,9 @@
     own_block.wait()
     prepare(0)
 
-    def await_next(k, carry):
-        arrive(GROUP + k)
-        return carry
-
-    lax.fori_loop(0, GROUP, await_next, 0)
+    arrive(GROUP + j)
+    for step in offsets:
+        arrive(GROUP + chip(*step))
 
     prepare(GROUP)
     for k in late:
@@ -230,13 +232,10 @@
             src_ref=src.at[here], dst_ref=dst.at[there], send_sem=send_sem, recv_sem=recv_sem.at[there],
             device_id={"dt": device}, device_id_type=MESH)
 
-    def spread(src, dst, send_sem, recv_sem):
-        def push(k, carry):
-            other = (j + k) & (GROUP - 1)
+    def spread(src, dst, send_sem, recv_sem, order):
+        for step in order:
+            other = chip(*step)
             piece(src, dst, send_sem, recv_sem, other, j, other).start()
-            return carry
-
-        lax.fori_loop(1, GROUP, push, 0)
         dst[pl.ds(j, 1)] = src[pl.ds(j, 1)]
 
     def take(src, dst, send_sem, recv_sem, source):
@@ -249,7 +248,7 @@
 
         lax.fori_loop(1, GROUP, left, 0)
 
-    spread(cs, xb, a1_send, a1_recv)
+    spread(cs, xb, a1_send, a1_recv, offsets[::-1])
 
     def sky_left(k, carry):
         sky_copy(own, j, {"obs": before}).wait_send()
@@ -257,11 +256,8 @@
 
     lax.fori_loop(0, sky_sends, sky_left, 0)
 
-    def take_series(k, carry):
-        take(cs, xb, a1_send, a1_recv, (j + k) & (GROUP - 1))
-        return carry
-
-    lax.fori_loop(1, GROUP, take_series, 0)
+    for step in offsets:
+        take(cs, xb, a1_send, a1_recv, chip(*step))
 
     def exact_left(high, low, x):
         xh, xl = split(x)
@@ -286,7 +282,7 @@
     filtered = jnp.concatenate([filtered[:128], filtered[128:]], axis=1)
     for i in range(GROUP):
         fs[i] = filtered[2 * i:2 * i + 2]
-    spread(fs, wb, a2_send, a2_recv)
+    spread(fs, wb, a2_send, a2_recv, offsets)
     all_left(cs, a1_send, xb, a1_recv)
 
     def scatter(k, carry):
@@ -336,6 +332,14 @@
             src_ref=s2.at[part, row], dst_ref=r2.at[part, slot], send_sem=r2_send,
             recv_sem=r2_recv.at[part, slot], device_id={"dt": row * NZ + z}, device_id_type=MESH)
 
+    def by_neighbour(part, side):
+        step = 1 - 2 * side
+        row = (y + step) & (NY - 1)
+        return pltpu.make_async_remote_copy(
+            src_ref=s2.at[part, (y + 2) & (NY - 1), :, :, pl.ds(side * (PIX // 2), PIX // 2)],
+            dst_ref=r4.at[part, side], send_sem=r4_send, recv_sem=r4_recv.at[part, side],
+            device_id={"dt": row * NZ + z}, device_id_type=MESH)
+
     def to_owner(other, slot):
         return pltpu.make_async_remote_copy(
             src_ref=s3.at[other], dst_ref=r3.at[slot], send_sem=r3_send, recv_sem=r3_recv.at[slot],
@@ -349,11 +353,18 @@
         for k, row in enumerate(turns):
             to_next(row, part).wait_recv()
             s2[part, row] = block(row, part)[...] + r1[part, row]
-            if k < NY - 1:
-                to_row(row, part, y).start()
+            if k == 0:
+                for side in range(2):
+                    by_neighbour(part, side).start()
+        for side in range(2):
+            row = (y + 1 - 2 * side) & (NY - 1)
+            lanes = slice(side * (PIX // 2), (side + 1) * (PIX // 2))
+            by_neighbour(part, side).wait_recv()
+            s2[part, row, :, :, lanes] = s2[part, row, :, :, lanes] + r4[part, side]
+            to_row(row, part, y).start()
     for part in halves:
         total = s2[part, y]
-        for row in turns[:NY - 1]:
+        for row in turns[1:NY - 1]:
             to_row(row, part, row).wait_recv()
             total = total + r2[part, row]
         for k in range(half):
@@ -377,8 +388,9 @@
     for part in range(2):
         for row in range(NY):
             to_next(row, part).wait_send()
-        for k in range(1, NY):
-            to_row((y + k) & (NY - 1), part, y).wait_send()
+        for side in range(2):
+            by_neighbour(part, side).wait_send()
+            to_row((y + 1 - 2 * side) & (NY - 1), part, y).wait_send()
     for k in range(1, NZ):
         to_owner((z + k) & (NZ - 1), z).wait_send()
 
@@ -413,10 +425,11 @@
             pltpu.VMEM((2, NY, 3, NZ // 2, PIX), f32),
             pltpu.VMEM((2, NY, 3, NZ // 2, PIX), f32),
             pltpu.VMEM((2, NY, 3, NZ // 2, PIX), f32),
+            pltpu.VMEM((2, 2, 3, NZ // 2, PIX // 2), f32),
             pltpu.VMEM((NZ, 3, PIX), f32),
             pltpu.VMEM((NZ, 3, PIX), f32),
-            dma((WINDOW,)), dma((GROUP,)), dma((GROUP,)), dma((2, NY)), dma((2, NY)), dma((NZ,)),
-            dma, dma, dma, dma, dma, dma,
+            dma((WINDOW,)), dma((GROUP,)), dma((GROUP,)), dma((2, NY)), dma((2, NY)), dma((2, 2)), dma((NZ,)),
+            dma, dma, dma, dma, dma, dma, dma,
         ],
         compiler_params=pltpu.CompilerParams(
             collective_id=0, has_side_effects=True, vmem_limit_bytes=60 << 20),

time: 128 us -> 127 us (level)
  no operation moved by 1% of the time
where the time goes in v4:
time: 127 us
  Pallas kernels  126 us (99%)
  local copies, waits for them, and re-layouts  1.29 us (1%)
    pallas_call x1, Pallas kernels, body(): pl.pallas_call(kernel, out_shape=jax.ShapeDtypeStruct((3, 1, PIX), f32),...  126 us

profile of v4, /device:TPU:6, one launch (start us, length us, event | category | flops | bytes accessed | tf_op | source)
XLA Modules:
  0.0 127.1 jit_solution(3321906764528779324)
XLA Ops:
  0.0 125.8 %mapmaker.1 = f32[3,1,512]{2,1,0:T(1,128)} custom-call(f32[3,1,512]{2,1,0:T(1,128)} %bitcast.3, s32[1,128,256]{2,1,0:T(8,128)} %refs_0_.1, s32[1,128,256]{2,1,0:T(8,128)} %refs_1_.1, f32[1,128,256]{2,1,0:T(8,128)} %refs_2_.1, s32[1,256]{1,0:T(1,128)} %refs_3_.1, s32[1,128]{1,0:T(1,128)} %refs_4_.1, bf16[1,128,128]{2,1,0:T(8,128)(2,1)} %refs_5_.1, ...), custom_call_target="tpu_custom_call" | custom-call | tf_op jit(solution)/shard_map/mapmaker/pallas_call | solution.py:403
  125.8 1.3 %copy.20 = f32[1,3,512]{2,0,1:T(1,128)} copy(f32[1,3,512]{2,0,1:T(1,128)} %bitcast.2) | data formatting | bytes 12288

commit v5 on v4

--- a/solution.py
+++ b/solution.py
@@ -192,11 +192,14 @@
     own_block.wait()
     prepare(0)
 
-    arrive(GROUP + j)
-    for step in offsets:
-        arrive(GROUP + chip(*step))
-
-    prepare(GROUP)
+    for dy in (0, 1, -1, 2):
+        for dz in sorted(range(1 - NZ // 2, NZ // 2 + 1), key=abs):
+            arrive(GROUP + chip(dy, dz))
+        first = pl.multiple_of(GROUP + ((y + dy) & (NY - 1)) * NZ, NZ)
+        for c in range(3):
+            high, low = split(tab[pl.ds(first, NZ), c, 0, :])
+            lhs[pl.ds(c * WINDOW + first, NZ), :] = high
+            lhs[pl.ds((3 + c) * WINDOW + first, NZ), :] = low
     for k in late:
         load(k).wait()
 

time: 127 us -> 127 us (level)
  no operation moved by 1% of the time
where the time goes in v5:
time: 127 us
  Pallas kernels  126 us (99%)
  local copies, waits for them, and re-layouts  1.29 us (1%)
    pallas_call x1, Pallas kernels, body(): pl.pallas_call(kernel, out_shape=jax.ShapeDtypeStruct((3, 1, PIX), f32),...  126 us

profile of v5, /device:TPU:6, one launch (start us, length us, event | category | flops | bytes accessed | tf_op | source)
XLA Modules:
  0.0 127.2 jit_solution(13046001139958154763)
XLA Ops:
  0.0 125.9 %mapmaker.1 = f32[3,1,512]{2,1,0:T(1,128)} custom-call(f32[3,1,512]{2,1,0:T(1,128)} %bitcast.3, s32[1,128,256]{2,1,0:T(8,128)} %refs_0_.1, s32[1,128,256]{2,1,0:T(8,128)} %refs_1_.1, f32[1,128,256]{2,1,0:T(8,128)} %refs_2_.1, s32[1,256]{1,0:T(1,128)} %refs_3_.1, s32[1,128]{1,0:T(1,128)} %refs_4_.1, bf16[1,128,128]{2,1,0:T(8,128)(2,1)} %refs_5_.1, ...), custom_call_target="tpu_custom_call" | custom-call | tf_op jit(solution)/shard_map/mapmaker/pallas_call | solution.py:406
  125.9 1.3 %copy.20 = f32[1,3,512]{2,0,1:T(1,128)} copy(f32[1,3,512]{2,0,1:T(1,128)} %bitcast.2) | data formatting | bytes 12288
